TPU v7x, 256 devices: a whole 4x4x8 slice. The times are simulated.
256 devices in a mesh: blk: 32 (over y_lo, z, core), uly: 8 (over y_hi, x).
Axes of the slice: x: 4, y: 4 (y_hi: 2, y_lo: 2; y = y_hi * 2 + y_lo), z: 8, core: 2. Of those that a mesh axis runs over, the one named last changes fastest.
Arguments:
- tokens: bfloat16 [32768, 5120], P(('blk', 'uly')), may hold values from -6 to 6
- query_base: bfloat16 [32768, 5120], P(('blk', 'uly')), may hold values from -9 to 9
- key_base: bfloat16 [32768, 5120], P(('blk', 'uly')), may hold values from -9 to 9
- value_base: bfloat16 [32768, 5120], P(('blk', 'uly')), may hold values from -6 to 6
- out_grad: bfloat16 [32768, 5120], P(('blk', 'uly')), may hold values from -0.059814453 to 0.059814453
- down_q: bfloat16 [5120, 64], replicated, may hold values from -0.078125 to 0.078125
- up_q: bfloat16 [64, 5120], replicated, may hold values from -0.75 to 0.75
- down_v: bfloat16 [5120, 64], replicated, may hold values from -0.078125 to 0.078125
- up_v: bfloat16 [64, 5120], replicated, may hold values from -0.75 to 0.75
Outputs:
- attended: bfloat16 [32768, 5120], P(('blk', 'uly'))
- grad_down_q: bfloat16 [5120, 64], replicated
- grad_up_q: bfloat16 [64, 5120], P(None, 'uly')
- grad_down_v: bfloat16 [5120, 64], replicated
- grad_up_v: bfloat16 [64, 5120], P(None, 'uly')
All inputs are finite; a program needn't handle non-finite values.
Results may differ from a plain program's by a relative error of at most 0.025.
Values may be sent and summed in bfloat16 or wider, within the bound.
No kernel may reach another device: no remote copies, remote signals or barrier semaphores. Data moves between devices by JAX's collectives and lax.ppermute only.
A program may use at most 128 MiB of HBM per device.

v0:
```python
import jax
import jax.numpy as jnp
from jax import lax
from jax.sharding import PartitionSpec as P

HEAD = 128


def passed_along(block, axis, distance):
    devices = range(lax.axis_size(axis))
    route = [(i - distance, i) for i in devices if i - distance in devices]
    return lax.ppermute(block, axis, route)


def inner(left, right):
    return lax.dot_general(
        left, right, (((0,), (0,)), ((), ())), preferred_element_type=jnp.float32
    )


def head_pass(query, keys, values, upstream, usable, scale):
    scores = jnp.dot(query, keys.T, preferred_element_type=jnp.float32) * scale
    scores = jnp.where(usable[None, :], scores, -jnp.inf)
    top = jnp.max(scores, axis=1, keepdims=True)
    total = jnp.sum(jnp.exp(scores - top), axis=1, keepdims=True)
    probs = jnp.exp(scores - top - jnp.log(total)).astype(jnp.bfloat16)
    attended = jnp.dot(probs, values, preferred_element_type=jnp.float32).astype(jnp.bfloat16)
    delta = jnp.sum(
        upstream.astype(jnp.float32) * attended.astype(jnp.float32), axis=1, keepdims=True
    )
    prob_grad = jnp.dot(upstream, values.T, preferred_element_type=jnp.float32)
    score_grad = (probs.astype(jnp.float32) * (prob_grad - delta)).astype(jnp.bfloat16)
    query_grad = (jnp.dot(score_grad, keys, preferred_element_type=jnp.float32) * scale).astype(
        jnp.bfloat16
    )
    value_terms = jnp.dot(probs.T, upstream, preferred_element_type=jnp.float32)
    return (attended, query_grad, value_terms)


def per_device(tokens, query_base, key_base, value_base, out_grad, down_q, up_q, down_v, up_v):
    low_q = jnp.dot(tokens, down_q, preferred_element_type=jnp.float32).astype(jnp.bfloat16)
    low_v = jnp.dot(tokens, down_v, preferred_element_type=jnp.float32).astype(jnp.bfloat16)
    query = (
        query_base.astype(jnp.float32) + jnp.dot(low_q, up_q, preferred_element_type=jnp.float32)
    ).astype(jnp.bfloat16)
    value = (
        value_base.astype(jnp.float32) + jnp.dot(low_v, up_v, preferred_element_type=jnp.float32)
    ).astype(jnp.bfloat16)
    query_h, keys_h, values_h, upstream_h = (
        lax.all_to_all(query, "uly", split_axis=1, concat_axis=0, tiled=True),
        lax.all_to_all(key_base, "uly", split_axis=1, concat_axis=0, tiled=True),
        lax.all_to_all(value, "uly", split_axis=1, concat_axis=0, tiled=True),
        lax.all_to_all(out_grad, "uly", split_axis=1, concat_axis=0, tiled=True),
    )
    rows = query_h.shape[0]
    width = query_h.shape[1]
    heads_here = width // HEAD
    scale = HEAD ** (-0.5)
    earlier = passed_along(jnp.stack([keys_h, values_h]), "blk", 1)
    keys_all = jnp.concatenate([earlier[0], keys_h], 0)
    values_all = jnp.concatenate([earlier[1], values_h], 0)
    column = jnp.arange(2 * rows)
    usable = jnp.logical_or(column >= rows, lax.axis_index("blk") > 0)

    def per_head(index, carry):
        attended, query_grad, own_terms, prior_terms = carry
        start = index * HEAD
        result = head_pass(
            lax.dynamic_slice_in_dim(query_h, start, HEAD, 1),
            lax.dynamic_slice_in_dim(keys_all, start, HEAD, 1),
            lax.dynamic_slice_in_dim(values_all, start, HEAD, 1),
            lax.dynamic_slice_in_dim(upstream_h, start, HEAD, 1),
            usable,
            scale,
        )
        attended = lax.dynamic_update_slice_in_dim(attended, result[0], start, 1)
        query_grad = lax.dynamic_update_slice_in_dim(query_grad, result[1], start, 1)
        prior_terms = lax.dynamic_update_slice_in_dim(prior_terms, result[2][:rows], start, 1)
        own_terms = lax.dynamic_update_slice_in_dim(own_terms, result[2][rows:], start, 1)
        return (attended, query_grad, own_terms, prior_terms)

    empty_half = jnp.zeros((rows, width), jnp.bfloat16)
    empty_full = jnp.zeros((rows, width), jnp.float32)
    attended_h, query_grad_h, own_terms, prior_terms = lax.fori_loop(
        0, heads_here, per_head, (empty_half, empty_half, empty_full, empty_full)
    )
    returned = passed_along(prior_terms, "blk", -1)
    value_grad_h = (own_terms + returned).astype(jnp.bfloat16)
    rank = down_q.shape[1]
    first_col = lax.axis_index("uly") * width
    attended, query_grad, value_grad = (
        lax.all_to_all(attended_h, "uly", split_axis=0, concat_axis=1, tiled=True),
        lax.all_to_all(query_grad_h, "uly", split_axis=0, concat_axis=1, tiled=True),
        lax.all_to_all(value_grad_h, "uly", split_axis=0, concat_axis=1, tiled=True),
    )
    lowrank = jnp.concatenate(
        [
            jnp.dot(query_grad, up_q.T, preferred_element_type=jnp.float32),
            jnp.dot(value_grad, up_v.T, preferred_element_type=jnp.float32),
        ],
        1,
    ).astype(jnp.bfloat16)
    down_terms = inner(tokens, lowrank)
    up_q_terms = inner(low_q, query_grad)
    up_v_terms = inner(low_v, value_grad)
    down_total, up_q_total, up_v_total = lax.psum(
        (down_terms, up_q_terms, up_v_terms), ("blk", "uly")
    )
    up_q_part = lax.dynamic_slice_in_dim(up_q_total, first_col, width, 1)
    up_v_part = lax.dynamic_slice_in_dim(up_v_total, first_col, width, 1)
    return (
        attended,
        down_total[:, :rank].astype(jnp.bfloat16),
        up_q_part.astype(jnp.bfloat16),
        down_total[:, rank:].astype(jnp.bfloat16),
        up_v_part.astype(jnp.bfloat16),
    )


def solution(mesh):
    return jax.shard_map(
        per_device,
        mesh=mesh,
        in_specs=(
            P(("blk", "uly"), None),
            P(("blk", "uly"), None),
            P(("blk", "uly"), None),
            P(("blk", "uly"), None),
            P(("blk", "uly"), None),
            P(),
            P(),
            P(),
            P(),
        ),
        out_specs=(P(("blk", "uly"), None), P(), P(None, "uly"), P(), P(None, "uly")),
        check_vma=False,
    )
```

profile of v0, /device:TPU:7, one launch (start us, length us, event | category | flops | bytes accessed | tf_op | source)
XLA Modules:
  0.0 464.2 jit_solution(9758977872020225476)
XLA Ops:
  6.5 6.8 %all-to-all-start.2 = ((bf16[128,8,640]{2,0,1:T(8,128)(2,1)}), bf16[128,8,640]{2,0,1:T(8,128)(2,1)S(1)}, u32[]{:S(2)}, u32[]{:S(2)}) async-start(bf16[128,8,640]{2,0,1:T(8,128)(2,1)} %bitcast.90), calls=%async_computation.2 | async-start | bytes 2621440 | tf_op jit(solution)/shard_map/all_to_all | solution.py:52
  13.3 2.5 copy.67
  15.8 15.6 %all-to-all-done.2 = bf16[128,8,640]{2,0,1:T(8,128)(2,1)S(1)} async-done(((bf16[128,8,640]{2,0,1:T(8,128)(2,1)}), bf16[128,8,640]{2,0,1:T(8,128)(2,1)S(1)}, u32[]{:S(2)}, u32[]{:S(2)}) %all-to-all-start.2) | async-done | bytes 1310752 | tf_op jit(solution)/shard_map/all_to_all | solution.py:52
  31.4 22.6 %all_to_all.133 = bf16[128,8,640]{2,0,1:T(8,128)(2,1)S(1)} all-to-all(bf16[128,8,640]{2,0,1:T(8,128)(2,1)} %bitcast.91), channel_id=1, replica_groups=mesh['blk'=32,'uly'=8] {'uly'}, dimensions={1} | all-to-all | bytes 2621440 | tf_op jit(solution)/shard_map/all_to_all | solution.py:51
  55.8 5.6 %collective-permute-start = (bf16[2,1024,640]{2,1,0:T(8,128)(2,1)}, bf16[2,1024,640]{2,1,0:T(8,128)(2,1)}, u32[]{:S(2)}, u32[]{:S(2)}) collective-permute-start(bf16[2,1024,640]{2,1,0:T(8,128)(2,1)} %pad_maximum_fusion), channel_id=1, source_target_pairs={{0,8},{8,16},{16,24},{24,32},{32,40},{40,48},{48,56},{56,64},{64,7... | collective-permute-start | bytes 7864328 | tf_op jit(solution)/shard_map/ppermute | solution.py:12
  61.5 2.5 copy.48
  64.0 6.0 %all-to-all-start.3 = ((bf16[128,8,640]{0,2,1:T(8,128)(2,1)}), bf16[128,8,640]{0,2,1:T(8,128)(2,1)}, u32[]{:S(2)}, u32[]{:S(2)}) async-start(bf16[128,8,640]{0,2,1:T(8,128)(2,1)} %bitcast.89), calls=%async_computation.3 | async-start | bytes 2621440 | tf_op jit(solution)/shard_map/all_to_all | solution.py:53
  73.5 34.2 %all-to-all-done.3 = bf16[128,8,640]{0,2,1:T(8,128)(2,1)} async-done(((bf16[128,8,640]{0,2,1:T(8,128)(2,1)}), bf16[128,8,640]{0,2,1:T(8,128)(2,1)}, u32[]{:S(2)}, u32[]{:S(2)}) %all-to-all-start.3) | async-done | bytes 1310752 | tf_op jit(solution)/shard_map/all_to_all | solution.py:53
  107.7 5.8 %all-to-all-start = ((bf16[128,8,640]{2,0,1:T(8,128)(2,1)}), bf16[128,8,640]{2,0,1:T(8,128)(2,1)}, u32[]{:S(2)}, u32[]{:S(2)}) async-start(bf16[128,8,640]{2,0,1:T(8,128)(2,1)} %bitcast.86), calls=%async_computation | async-start | bytes 2621440 | tf_op jit(solution)/shard_map/all_to_all | solution.py:50
  113.5 2.4 copy.49
  118.1 6.8 %pad_maximum_fusion.1 = (bf16[2048,640]{1,0:T(8,128)(2,1)}, bf16[2048,640]{1,0:T(8,128)(2,1)}) fusion(bf16[1024,640]{1,0:T(8,128)(2,1)S(1)} %bitcast.77, bf16[1024,640]{1,0:T(8,128)(2,1)S(1)} %get-tuple-element.289, bf16[1024,640]{1,0:T(8,128)(2,1)S(1)} %bitcast.75, bf16[1024,640]{1,0:T(8,128)(2,1)S(1)} %get-tuple-element.288), kind=kLoop, calls=%fused_computation.33 | loop fusion | flops 10485760 | bytes 10485760 | tf_op jit(solution)/shard_map/concatenate | solution.py:60
  124.8 6.9 %all-to-all-done = bf16[128,8,640]{2,0,1:T(8,128)(2,1)} async-done(((bf16[128,8,640]{2,0,1:T(8,128)(2,1)}), bf16[128,8,640]{2,0,1:T(8,128)(2,1)}, u32[]{:S(2)}, u32[]{:S(2)}) %all-to-all-start) | async-done | bytes 1310752 | tf_op jit(solution)/shard_map/all_to_all | solution.py:50
  136.3 103.0 %while.20 = (s32[]{:T(128)}, bf16[1024,640]{1,0:T(8,128)(2,1)S(1)}, bf16[1024,640]{1,0:T(8,128)(2,1)}, f32[1024,640]{1,0:T(8,128)}, f32[1024,640]{1,0:T(8,128)},...) while((s32[]{:T(128)}, bf16[1024,640]{1,0:T(8,128)(2,1)S(1)}, ...), condition=%wide.region_4.5_spmd.clone, body=%wide.region_0.4_spmd.clone.sunk | while | flops 2718827520 | bytes 67680992 | solution.py:84
  136.3 2.6 fusion.67
  138.9 2.2 exponential_reduce_fusion.2
  141.1 2.3 exponential_convert_fusion.2
  147.2 3.8 multiply_reduce_fusion.2
  151.0 5.6 %fusion.68 = bf16[1024,640]{1,0:T(8,128)(2,1)} fusion(bf16[1024,640]{1,0:T(8,128)(2,1)} %get-tuple-element.383, s32[]{:T(128)S(6)} %select_n.43, bf16[1024,2048]{1,0:T(8,128)(2,1)} %copy-done.1, bf16[1024,128]{1,0:T(8,128)(2,1)S(1)} %constant_dynamic-slice_fusion.2, f32[1024]{0:T(1024)S(1)} %get-tuple-element.364, ...), kind=kOutput, calls=%fused_computation.10.clone.1 | convolution fusion | flops 1082392576 | bytes 5772800 | tf_op jit(solution)/shard_map/while/body/eval_jaxpr/dot_general | solution.py:33
  157.0 2.6 fusion.67
  159.5 2.2 exponential_reduce_fusion.2
  161.8 2.3 exponential_convert_fusion.2
  167.8 3.8 multiply_reduce_fusion.2
  171.6 5.6 %fusion.68 = bf16[1024,640]{1,0:T(8,128)(2,1)} fusion(bf16[1024,640]{1,0:T(8,128)(2,1)} %get-tuple-element.383, s32[]{:T(128)S(6)} %select_n.43, bf16[1024,2048]{1,0:T(8,128)(2,1)} %copy-done.1, bf16[1024,128]{1,0:T(8,128)(2,1)S(1)} %constant_dynamic-slice_fusion.2, f32[1024]{0:T(1024)S(1)} %get-tuple-element.364, ...), kind=kOutput, calls=%fused_computation.10.clone.1 | convolution fusion | flops 1082392576 | bytes 5772800 | tf_op jit(solution)/shard_map/while/body/eval_jaxpr/dot_general | solution.py:33
  177.6 2.6 fusion.67
  180.1 2.2 exponential_reduce_fusion.2
  182.4 2.3 exponential_convert_fusion.2
  188.4 3.8 multiply_reduce_fusion.2
  192.2 5.6 %fusion.68 = bf16[1024,640]{1,0:T(8,128)(2,1)} fusion(bf16[1024,640]{1,0:T(8,128)(2,1)} %get-tuple-element.383, s32[]{:T(128)S(6)} %select_n.43, bf16[1024,2048]{1,0:T(8,128)(2,1)} %copy-done.1, bf16[1024,128]{1,0:T(8,128)(2,1)S(1)} %constant_dynamic-slice_fusion.2, f32[1024]{0:T(1024)S(1)} %get-tuple-element.364, ...), kind=kOutput, calls=%fused_computation.10.clone.1 | convolution fusion | flops 1082392576 | bytes 5772800 | tf_op jit(solution)/shard_map/while/body/eval_jaxpr/dot_general | solution.py:33
  198.2 2.6 fusion.67
  203.0 2.3 exponential_convert_fusion.2
  209.0 3.8 multiply_reduce_fusion.2
  212.8 5.6 %fusion.68 = bf16[1024,640]{1,0:T(8,128)(2,1)} fusion(bf16[1024,640]{1,0:T(8,128)(2,1)} %get-tuple-element.383, s32[]{:T(128)S(6)} %select_n.43, bf16[1024,2048]{1,0:T(8,128)(2,1)} %copy-done.1, bf16[1024,128]{1,0:T(8,128)(2,1)S(1)} %constant_dynamic-slice_fusion.2, f32[1024]{0:T(1024)S(1)} %get-tuple-element.364, ...), kind=kOutput, calls=%fused_computation.10.clone.1 | convolution fusion | flops 1082392576 | bytes 5772800 | tf_op jit(solution)/shard_map/while/body/eval_jaxpr/dot_general | solution.py:33
  218.7 2.6 fusion.67
  221.3 2.2 exponential_reduce_fusion.2
  223.5 2.3 exponential_convert_fusion.2
  229.6 3.8 multiply_reduce_fusion.2
  233.4 5.6 %fusion.68 = bf16[1024,640]{1,0:T(8,128)(2,1)} fusion(bf16[1024,640]{1,0:T(8,128)(2,1)} %get-tuple-element.383, s32[]{:T(128)S(6)} %select_n.43, bf16[1024,2048]{1,0:T(8,128)(2,1)} %copy-done.1, bf16[1024,128]{1,0:T(8,128)(2,1)S(1)} %constant_dynamic-slice_fusion.2, f32[1024]{0:T(1024)S(1)} %get-tuple-element.364, ...), kind=kOutput, calls=%fused_computation.10.clone.1 | convolution fusion | flops 1082392576 | bytes 5772800 | tf_op jit(solution)/shard_map/while/body/eval_jaxpr/dot_general | solution.py:33
  239.3 2.4 collective-permute-start.1
  241.7 24.9 %all_to_all.134 = bf16[8,128,640]{2,1,0:T(8,128)(2,1)} all-to-all(bf16[8,128,640]{2,1,0:T(8,128)(2,1)} %bitcast.88), channel_id=1, replica_groups=mesh['blk'=32,'uly'=8] {'uly'}, dimensions={0} | all-to-all | bytes 2621440 | tf_op jit(solution)/shard_map/all_to_all | solution.py:93
  266.7 5.5 %all-to-all-start.4 = ((bf16[8,128,640]{2,1,0:T(8,128)(2,1)}), bf16[8,128,640]{2,1,0:T(8,128)(2,1)S(1)}, u32[]{:S(2)}, u32[]{:S(2)}) async-start(bf16[8,128,640]{2,1,0:T(8,128)(2,1)} %bitcast.87), calls=%async_computation.4 | async-start | bytes 2621440 | tf_op jit(solution)/shard_map/all_to_all | solution.py:92
  272.6 3.8 add_convert_fusion
  276.4 12.2 %all-to-all-done.4 = bf16[8,128,640]{2,1,0:T(8,128)(2,1)S(1)} async-done(((bf16[8,128,640]{2,1,0:T(8,128)(2,1)}), bf16[8,128,640]{2,1,0:T(8,128)(2,1)S(1)}, u32[]{:S(2)}, u32[]{:S(2)}) %all-to-all-start.4) | async-done | bytes 1310752 | tf_op jit(solution)/shard_map/all_to_all | solution.py:92
  288.7 7.9 %all-to-all-start.6 = ((bf16[8,128,640]{2,1,0:T(8,128)(2,1)}), bf16[8,128,640]{2,1,0:T(8,128)(2,1)}, u32[]{:S(2)}, u32[]{:S(2)}) async-start(bf16[8,128,640]{2,1,0:T(8,128)(2,1)} %bitcast.93), calls=%async_computation.6 | async-start | bytes 2621440 | tf_op jit(solution)/shard_map/all_to_all | solution.py:94
  299.9 2.5 copy.53
  302.4 2.4 copy.56
  305.2 9.5 %all-to-all-done.6 = bf16[8,128,640]{2,1,0:T(8,128)(2,1)} async-done(((bf16[8,128,640]{2,1,0:T(8,128)(2,1)}), bf16[8,128,640]{2,1,0:T(8,128)(2,1)}, u32[]{:S(2)}, u32[]{:S(2)}) %all-to-all-start.6) | async-done | bytes 1310752 | tf_op jit(solution)/shard_map/all_to_all | solution.py:94
  320.5 139.1 %all-reduce.2 = (bf16[5120,128]{0,1:T(8,128)(2,1)}, bf16[64,5120]{1,0:T(8,128)(2,1)S(1)}, bf16[64,5120]{1,0:T(8,128)(2,1)}) all-reduce(f32[5120,128]{0,1:T(8,128)} %convolution_bitcast_fusion, f32[64,5120]{1,0:T(8,128)S(1)} %copy-done.4, f32[64,5120]{1,0:T(8,128)} %fusion.28), channel_id=1, replica_groups=mesh['blk'=32,'uly'=8] {'blk','uly'}, use_global_device_ids=true, to_apply=%region_5.6 | all-reduce | flops 1310720 | bytes 7864320 | tf_op jit(solution)/shard_map/psum | solution.py:106
  459.6 2.4 fusion.25
  (96 shorter events, 52.1 us)
Async XLA Ops:
  0.6 1.3 copy-start
  0.6 3.0 copy-start.10
  6.5 24.9 %all-to-all-start.2 = ((bf16[128,8,640]{2,0,1:T(8,128)(2,1)}), bf16[128,8,640]{2,0,1:T(8,128)(2,1)S(1)}, u32[]{:S(2)}, u32[]{:S(2)}) async-start(bf16[128,8,640]{2,0,1:T(8,128)(2,1)} %bitcast.90), calls=%async_computation.2 | async-start | bytes 2621440 | tf_op jit(solution)/shard_map/all_to_all | solution.py:52
  53.9 1.9 copy-start.2
  55.8 60.1 %collective-permute-start = (bf16[2,1024,640]{2,1,0:T(8,128)(2,1)}, bf16[2,1024,640]{2,1,0:T(8,128)(2,1)}, u32[]{:S(2)}, u32[]{:S(2)}) collective-permute-start(bf16[2,1024,640]{2,1,0:T(8,128)(2,1)} %pad_maximum_fusion), channel_id=1, source_target_pairs={{0,8},{8,16},{16,24},{24,32},{32,40},{40,48},{48,56},{56,64},{64,7... | collective-permute-start | bytes 7864328 | tf_op jit(solution)/shard_map/ppermute | solution.py:12
  64.0 7.8 %copy-start.7 = (bf16[64,5120]{1,0:T(8,128)(2,1)S(1)}, bf16[64,5120]{1,0:T(8,128)(2,1)}, u32[]{:S(2)}) copy-start(bf16[64,5120]{1,0:T(8,128)(2,1)} %param.17) | copy-start | bytes 1966084
  64.0 43.7 %all-to-all-start.3 = ((bf16[128,8,640]{0,2,1:T(8,128)(2,1)}), bf16[128,8,640]{0,2,1:T(8,128)(2,1)}, u32[]{:S(2)}, u32[]{:S(2)}) async-start(bf16[128,8,640]{0,2,1:T(8,128)(2,1)} %bitcast.89), calls=%async_computation.3 | async-start | bytes 2621440 | tf_op jit(solution)/shard_map/all_to_all | solution.py:53
  70.0 1.8 copy-start.11
  107.7 24.0 %all-to-all-start = ((bf16[128,8,640]{2,0,1:T(8,128)(2,1)}), bf16[128,8,640]{2,0,1:T(8,128)(2,1)}, u32[]{:S(2)}, u32[]{:S(2)}) async-start(bf16[128,8,640]{2,0,1:T(8,128)(2,1)} %bitcast.86), calls=%async_computation | async-start | bytes 2621440 | tf_op jit(solution)/shard_map/all_to_all | solution.py:50
  116.0 2.1 copy-start.3
  143.4 2.5 copy-start.1
  164.0 2.5 copy-start.1
  184.6 2.5 copy-start.1
  205.2 2.5 copy-start.1
  225.8 2.5 copy-start.1
  239.3 27.4 %copy-start.6 = (bf16[1024,640]{1,0:T(8,128)(2,1)}, bf16[1024,640]{1,0:T(8,128)(2,1)S(1)}, u32[]{:S(2)}) copy-start(bf16[1024,640]{1,0:T(8,128)(2,1)S(1)} %get-tuple-element.177) | copy-start | bytes 3932164
  239.3 33.3 %collective-permute-start.1 = (f32[1024,640]{1,0:T(8,128)}, f32[1024,640]{1,0:T(8,128)}, u32[]{:S(2)}, u32[]{:S(2)}) collective-permute-start(f32[1024,640]{1,0:T(8,128)} %get-tuple-element.180), channel_id=1, source_target_pairs={{8,0},{16,8},{24,16},{32,24},{40,32},{48,40},{56,48},{64,56},{72,6... | collective-permute-start | bytes 7864328 | tf_op jit(solution)/shard_map/ppermute | solution.py:12
  266.7 22.0 %all-to-all-start.4 = ((bf16[8,128,640]{2,1,0:T(8,128)(2,1)}), bf16[8,128,640]{2,1,0:T(8,128)(2,1)S(1)}, u32[]{:S(2)}, u32[]{:S(2)}) async-start(bf16[8,128,640]{2,1,0:T(8,128)(2,1)} %bitcast.87), calls=%async_computation.4 | async-start | bytes 2621440 | tf_op jit(solution)/shard_map/all_to_all | solution.py:92
  288.7 7.9 %copy-start.5 = (bf16[8,128,640]{2,1,0:T(8,128)(2,1)}, bf16[8,128,640]{2,1,0:T(8,128)(2,1)S(1)}, u32[]{:S(2)}) copy-start(bf16[8,128,640]{2,1,0:T(8,128)(2,1)S(1)} %all-to-all-done.4) | copy-start | bytes 3932164
  288.7 26.1 %all-to-all-start.6 = ((bf16[8,128,640]{2,1,0:T(8,128)(2,1)}), bf16[8,128,640]{2,1,0:T(8,128)(2,1)}, u32[]{:S(2)}, u32[]{:S(2)}) async-start(bf16[8,128,640]{2,1,0:T(8,128)(2,1)} %bitcast.93), calls=%async_computation.6 | async-start | bytes 2621440 | tf_op jit(solution)/shard_map/all_to_all | solution.py:94
  299.9 4.9 %copy-start.8 = (bf16[64,5120]{1,0:T(8,128)(2,1)S(1)}, bf16[64,5120]{1,0:T(8,128)(2,1)}, u32[]{:S(2)}) copy-start(bf16[64,5120]{1,0:T(8,128)(2,1)} %param.17) | copy-start | bytes 1966084
  305.2 11.3 %copy-start.9 = (bf16[64,5120]{1,0:T(8,128)(2,1)S(1)}, bf16[64,5120]{1,0:T(8,128)(2,1)}, u32[]{:S(2)}) copy-start(bf16[64,5120]{1,0:T(8,128)(2,1)} %param.19) | copy-start | bytes 1966084
  318.5 2.0 copy-start.4
where the time goes:
time: 466 us; the launch traced here: 464 us
  blocking collectives  187 us (40%)
  waiting for transfers between devices  78.9 us (17%)
  matrix products  78.2 us (17%)
  local copies, waits for them, and re-layouts  44.3 us (10%)
  starting transfers between devices  40.1 us (9%)
  other arithmetic  34.9 us (7%)
    psum x1, blocking collectives, per_device(): lax.psum((down_terms, up_q_terms, up_v_terms), ('blk', 'uly'))  139 us
    all_to_all x1, waiting for transfers between devices, per_device(): lax.all_to_all(out_grad, 'uly', split_axis=1, concat_axis=0, tiled=True)  34.2 us
    dot_general x5, matrix products, head_pass(): jnp.dot(score_grad, keys, preferred_element_type=jnp.float32) * scale  28.2 us
    all_to_all x1, blocking collectives, per_device(): lax.all_to_all(query_grad_h, 'uly', split_axis=0, concat_axis=1, tiled=True)  24.9 us
    all_to_all x1, blocking collectives, per_device(): lax.all_to_all(key_base, 'uly', split_axis=1, concat_axis=0, tiled=True)  22.6 us
    dot_general x5, matrix products, head_pass(): jnp.dot(probs, values, preferred_element_type=jnp.float32)  19.2 us
    all_to_all x1, waiting for transfers between devices, per_device(): lax.all_to_all(value, 'uly', split_axis=1, concat_axis=0, tiled=True)  15.6 us
    dot_general x5, matrix products, head_pass(): scores = jnp.dot(query, keys.T, preferred_element_type=jnp.float32) * scale  12.8 us
  transfers between devices with their start and end apart: 7, of which 6 were waited for; matrix products, arithmetic and copies ran while one was open for 7% of the time, Pallas kernels for 0%

commit v1 on v0

--- a/solution.py
+++ b/solution.py
@@ -104,7 +104,7 @@
     up_q_terms = inner(low_q, query_grad)
     up_v_terms = inner(low_v, value_grad)
     down_total, up_q_total, up_v_total = lax.psum(
-        (down_terms, up_q_terms, up_v_terms), ("blk", "uly")
+        lax.psum((down_terms, up_q_terms, up_v_terms), "blk"), "uly"
     )
     up_q_part = lax.dynamic_slice_in_dim(up_q_total, first_col, width, 1)
     up_v_part = lax.dynamic_slice_in_dim(up_v_total, first_col, width, 1)

time: 466 us -> 669 us (1.44)
  waiting for transfers between devices: 78.9 us -> 319 us
  blocking collectives: 187 us -> 130 us
  between operations: 0.8 us -> 14.2 us
    psum x0 -> x1, waiting for transfers between devices: none -> 218 us  [per_device(): lax.psum((down_terms, up_q_terms, up_v_terms), 'blk')]
    psum x1, blocking collectives: 139 us -> 107 us  [per_device(): lax.psum(lax.psum((down_terms, up_q_terms, up_v_terms), 'blk'), 'uly')]
    all_to_all x1 -> x0, blocking collectives: 24.9 us -> none  [per_device(): lax.all_to_all(query_grad_h, 'uly', split_axis=0, concat_axis=1, tiled=True)]
    ppermute x2, waiting for transfers between devices: 0.45 us -> 25 us  [passed_along(): return lax.ppermute(block, axis, route)]
  transfers between devices with their start and end apart: 7 -> 9, of which waited for: 6 -> 7; matrix products, arithmetic and copies ran while one was open for 7% -> 5% of each run, Pallas kernels for 0% -> 0%
where the time goes in v1:
time: 669 us; the launch traced here: 663 us
  waiting for transfers between devices  319 us (48%)
  blocking collectives  130 us (19%)
  matrix products  78.2 us (12%)
  starting transfers between devices  44.5 us (7%)
  local copies, waits for them, and re-layouts  42 us (6%)
  other arithmetic  35 us (5%)
  between operations  14.2 us (2%)
    psum x1, waiting for transfers between devices, per_device(): lax.psum((down_terms, up_q_terms, up_v_terms), 'blk')  218 us
    psum x1, blocking collectives, per_device(): lax.psum(lax.psum((down_terms, up_q_terms, up_v_terms), 'blk'), 'uly')  107 us
    all_to_all x1, waiting for transfers between devices, per_device(): lax.all_to_all(out_grad, 'uly', split_axis=1, concat_axis=0, tiled=True)  34.2 us
    dot_general x5, matrix products, head_pass(): jnp.dot(score_grad, keys, preferred_element_type=jnp.float32) * scale  28.2 us
    ppermute x2, waiting for transfers between devices, passed_along(): return lax.ppermute(block, axis, route)  25 us
    all_to_all x1, blocking collectives, per_device(): lax.all_to_all(key_base, 'uly', split_axis=1, concat_axis=0, tiled=True)  22.6 us
    dot_general x5, matrix products, head_pass(): jnp.dot(probs, values, preferred_element_type=jnp.float32)  19.2 us
    all_to_all x1, waiting for transfers between devices, per_device(): lax.all_to_all(value, 'uly', split_axis=1, concat_axis=0, tiled=True)  15.6 us
  transfers between devices with their start and end apart: 9, of which 7 were waited for; matrix products, arithmetic and copies ran while one was open for 5% of the time, Pallas kernels for 0%

profile of v1, /device:TPU:7, one launch (start us, length us, event | category | flops | bytes accessed | tf_op | source)
XLA Modules:
  0.0 663.3 jit_solution(13912225079041169830)
XLA Ops:
  13.0 6.8 %all-to-all-start.2 = ((bf16[128,8,640]{2,0,1:T(8,128)(2,1)}), bf16[128,8,640]{2,0,1:T(8,128)(2,1)S(1)}, u32[]{:S(2)}, u32[]{:S(2)}) async-start(bf16[128,8,640]{2,0,1:T(8,128)(2,1)} %bitcast.90), calls=%async_computation.2 | async-start | bytes 2621440 | tf_op jit(solution)/shard_map/all_to_all | solution.py:52
  19.8 2.5 copy.67
  22.3 15.6 %all-to-all-done.2 = bf16[128,8,640]{2,0,1:T(8,128)(2,1)S(1)} async-done(((bf16[128,8,640]{2,0,1:T(8,128)(2,1)}), bf16[128,8,640]{2,0,1:T(8,128)(2,1)S(1)}, u32[]{:S(2)}, u32[]{:S(2)}) %all-to-all-start.2) | async-done | bytes 1310752 | tf_op jit(solution)/shard_map/all_to_all | solution.py:52
  37.9 22.6 %all_to_all.133 = bf16[128,8,640]{2,0,1:T(8,128)(2,1)S(1)} all-to-all(bf16[128,8,640]{2,0,1:T(8,128)(2,1)} %bitcast.91), channel_id=1, replica_groups=mesh['blk'=32,'uly'=8] {'uly'}, dimensions={1} | all-to-all | bytes 2621440 | tf_op jit(solution)/shard_map/all_to_all | solution.py:51
  62.4 5.6 collective-permute-start
  68.0 2.5 copy.48
  70.5 6.0 all-to-all-start.3
  80.0 34.2 %all-to-all-done.3 = bf16[128,8,640]{0,2,1:T(8,128)(2,1)} async-done(((bf16[128,8,640]{0,2,1:T(8,128)(2,1)}), bf16[128,8,640]{0,2,1:T(8,128)(2,1)}, u32[]{:S(2)}, u32[]{:S(2)}) %all-to-all-start.3) | async-done | bytes 1310752 | tf_op jit(solution)/shard_map/all_to_all | solution.py:53
  114.2 5.8 all-to-all-start
  120.0 2.4 copy.49
  124.6 6.7 %pad_maximum_fusion.1 = (bf16[2048,640]{1,0:T(8,128)(2,1)}, bf16[2048,640]{1,0:T(8,128)(2,1)}) fusion(bf16[1024,640]{1,0:T(8,128)(2,1)S(1)} %bitcast.77, bf16[1024,640]{1,0:T(8,128)(2,1)S(1)} %get-tuple-element.292, bf16[1024,640]{1,0:T(8,128)(2,1)S(1)} %bitcast.75, bf16[1024,640]{1,0:T(8,128)(2,1)S(1)} %get-tuple-element.291), kind=kLoop, calls=%fused_computation.33 | loop fusion | flops 10485760 | bytes 10485760 | tf_op jit(solution)/shard_map/concatenate | solution.py:60
  131.3 6.9 %all-to-all-done = bf16[128,8,640]{2,0,1:T(8,128)(2,1)} async-done(((bf16[128,8,640]{2,0,1:T(8,128)(2,1)}), bf16[128,8,640]{2,0,1:T(8,128)(2,1)}, u32[]{:S(2)}, u32[]{:S(2)}) %all-to-all-start) | async-done | bytes 1310752 | tf_op jit(solution)/shard_map/all_to_all | solution.py:50
  142.8 103.0 %while.20 = (s32[]{:T(128)}, bf16[1024,640]{1,0:T(8,128)(2,1)S(1)}, bf16[1024,640]{1,0:T(8,128)(2,1)}, f32[1024,640]{1,0:T(8,128)}, f32[1024,640]{1,0:T(8,128)},...) while((s32[]{:T(128)}, bf16[1024,640]{1,0:T(8,128)(2,1)S(1)}, ...), condition=%wide.region_4.5_spmd.clone, body=%wide.region_0.4_spmd.clone.sunk | while | flops 2718827520 | bytes 67680992 | solution.py:84
  142.8 2.6 fusion.67
  145.4 2.2 exponential_reduce_fusion.2
  147.6 2.3 exponential_convert_fusion.2
  153.7 3.8 multiply_reduce_fusion.2
  157.5 5.6 fusion.68
  163.4 2.6 fusion.67
  166.0 2.2 exponential_reduce_fusion.2
  168.2 2.3 exponential_convert_fusion.2
  174.2 3.8 multiply_reduce_fusion.2
  178.1 5.6 fusion.68
  184.0 2.6 fusion.67
  186.6 2.2 exponential_reduce_fusion.2
  188.8 2.3 exponential_convert_fusion.2
  194.8 3.8 multiply_reduce_fusion.2
  198.6 5.6 fusion.68
  204.6 2.6 fusion.67
  207.1 2.2 exponential_reduce_fusion.2
  209.4 2.3 exponential_convert_fusion.2
  215.5 3.8 multiply_reduce_fusion.2
  219.3 5.6 fusion.68
  225.2 2.6 fusion.67
  230.0 2.3 exponential_convert_fusion.2
  236.1 3.8 multiply_reduce_fusion.2
  239.9 5.6 fusion.68
  245.8 2.4 collective-permute-start.1
  248.2 5.9 all-to-all-start.5
  254.2 25.0 %collective-permute-done.1 = f32[1024,640]{1,0:T(8,128)} collective-permute-done((f32[1024,640]{1,0:T(8,128)}, f32[1024,640]{1,0:T(8,128)}, u32[]{:S(2)}, u32[]{:S(2)}) %collective-permute-start.1) | collective-permute-done | bytes 2621472 | tf_op jit(solution)/shard_map/ppermute | solution.py:12
  279.1 3.9 add_convert_fusion
  283.0 6.4 all-to-all-start.6
  293.2 7.5 %all-to-all-done.6 = bf16[8,128,640]{2,1,0:T(8,128)(2,1)} async-done(((bf16[8,128,640]{2,1,0:T(8,128)(2,1)}), bf16[8,128,640]{2,1,0:T(8,128)(2,1)}, u32[]{:S(2)}, u32[]{:S(2)}) %all-to-all-start.6) | async-done | bytes 1310752 | tf_op jit(solution)/shard_map/all_to_all | solution.py:94
  306.6 5.6 all-to-all-start.4
  312.1 11.2 %all-to-all-done.4 = bf16[8,128,640]{2,1,0:T(8,128)(2,1)S(1)} async-done(((bf16[8,128,640]{2,1,0:T(8,128)(2,1)}), bf16[8,128,640]{2,1,0:T(8,128)(2,1)S(1)}, u32[]{:S(2)}, u32[]{:S(2)}) %all-to-all-start.4) | async-done | bytes 1310752 | tf_op jit(solution)/shard_map/all_to_all | solution.py:92
  324.8 2.4 copy.56
  327.3 218.5 %all-reduce.5.cloned.1.call-done = (f32[5120,128]{0,1:T(8,128)}, f32[64,5120]{1,0:T(8,128)}, f32[64,5120]{1,0:T(8,128)}) async-done(((f32[5120,128]{0,1:T(8,128)}, f32[64,5120]{1,0:T(8,128)}, f32[64,5120]{1,0:T(8,128)}), (f32[5120,128]{0,1:T(8,128)}, f32[64,5120]{1,0:T(8,128)}, f32[64,5120]{1,0:T(8,128)})) %all-reduce.5.cloned.1.call-update) | async-done | bytes 5242896 | tf_op jit(solution)/shard_map/psum | solution.py:107
  545.7 107.4 %all-reduce.6 = (bf16[5120,128]{0,1:T(8,128)(2,1)S(1)}, bf16[64,5120]{1,0:T(8,128)(2,1)S(1)}, bf16[64,5120]{1,0:T(8,128)(2,1)}) all-reduce(f32[5120,128]{0,1:T(8,128)} %get-tuple-element.279, f32[64,5120]{1,0:T(8,128)} %get-tuple-element.280, f32[64,5120]{1,0:T(8,128)} %get-tuple-element.281), channel_id=1, replica_groups=mesh['blk'=32,'uly'=8] {'uly'}, use_global_device_ids=true, to_apply=%region_6.7 | all-reduce | flops 1310720 | bytes 7864320 | tf_op jit(solution)/shard_map/psum | solution.py:106
  (98 shorter events, 54.3 us)
Async XLA Ops:
  7.2 1.3 copy-start
  7.2 3.0 copy-start.9
  13.0 24.9 %all-to-all-start.2 = ((bf16[128,8,640]{2,0,1:T(8,128)(2,1)}), bf16[128,8,640]{2,0,1:T(8,128)(2,1)S(1)}, u32[]{:S(2)}, u32[]{:S(2)}) async-start(bf16[128,8,640]{2,0,1:T(8,128)(2,1)} %bitcast.90), calls=%async_computation.2 | async-start | bytes 2621440 | tf_op jit(solution)/shard_map/all_to_all | solution.py:52
  60.5 1.9 copy-start.2
  62.4 60.1 %collective-permute-start = (bf16[2,1024,640]{2,1,0:T(8,128)(2,1)}, bf16[2,1024,640]{2,1,0:T(8,128)(2,1)}, u32[]{:S(2)}, u32[]{:S(2)}) collective-permute-start(bf16[2,1024,640]{2,1,0:T(8,128)(2,1)} %pad_maximum_fusion), channel_id=1, source_target_pairs={{0,8},{8,16},{16,24},{24,32},{32,40},{40,48},{48,56},{56,64},{64,7... | collective-permute-start | bytes 7864328 | tf_op jit(solution)/shard_map/ppermute | solution.py:12
  70.5 7.8 %copy-start.6 = (bf16[64,5120]{1,0:T(8,128)(2,1)S(1)}, bf16[64,5120]{1,0:T(8,128)(2,1)}, u32[]{:S(2)}) copy-start(bf16[64,5120]{1,0:T(8,128)(2,1)} %param.17) | copy-start | bytes 1966084
  70.5 43.7 %all-to-all-start.3 = ((bf16[128,8,640]{0,2,1:T(8,128)(2,1)}), bf16[128,8,640]{0,2,1:T(8,128)(2,1)}, u32[]{:S(2)}, u32[]{:S(2)}) async-start(bf16[128,8,640]{0,2,1:T(8,128)(2,1)} %bitcast.89), calls=%async_computation.3 | async-start | bytes 2621440 | tf_op jit(solution)/shard_map/all_to_all | solution.py:53
  76.5 1.8 copy-start.10
  114.2 24.0 %all-to-all-start = ((bf16[128,8,640]{2,0,1:T(8,128)(2,1)}), bf16[128,8,640]{2,0,1:T(8,128)(2,1)}, u32[]{:S(2)}, u32[]{:S(2)}) async-start(bf16[128,8,640]{2,0,1:T(8,128)(2,1)} %bitcast.85), calls=%async_computation | async-start | bytes 2621440 | tf_op jit(solution)/shard_map/all_to_all | solution.py:50
  122.5 2.1 copy-start.3
  149.9 2.5 copy-start.1
  170.5 2.5 copy-start.1
  191.1 2.5 copy-start.1
  211.6 2.5 copy-start.1
  232.3 2.5 copy-start.1
  245.8 2.4 copy-start.5
  245.8 33.3 %collective-permute-start.1 = (f32[1024,640]{1,0:T(8,128)}, f32[1024,640]{1,0:T(8,128)}, u32[]{:S(2)}, u32[]{:S(2)}) collective-permute-start(f32[1024,640]{1,0:T(8,128)} %get-tuple-element.180), channel_id=1, source_target_pairs={{8,0},{16,8},{24,16},{32,24},{40,32},{48,40},{56,48},{64,56},{72,6... | collective-permute-start | bytes 7864328 | tf_op jit(solution)/shard_map/ppermute | solution.py:12
  248.2 34.8 %all-to-all-start.5 = ((bf16[8,128,640]{2,1,0:T(8,128)(2,1)}), bf16[8,128,640]{2,1,0:T(8,128)(2,1)S(1)}, u32[]{:S(2)}, u32[]{:S(2)}) async-start(bf16[8,128,640]{2,1,0:T(8,128)(2,1)} %bitcast.88), calls=%async_computation.5 | async-start | bytes 2621440 | tf_op jit(solution)/shard_map/all_to_all | solution.py:93
  283.0 6.4 copy-start.4
  283.0 8.2 %copy-start.7 = (bf16[64,5120]{1,0:T(8,128)(2,1)S(1)}, bf16[64,5120]{1,0:T(8,128)(2,1)}, u32[]{:S(2)}) copy-start(bf16[64,5120]{1,0:T(8,128)(2,1)} %param.17) | copy-start | bytes 1966084
  283.0 17.7 %all-to-all-start.6 = ((bf16[8,128,640]{2,1,0:T(8,128)(2,1)}), bf16[8,128,640]{2,1,0:T(8,128)(2,1)}, u32[]{:S(2)}, u32[]{:S(2)}) async-start(bf16[8,128,640]{2,1,0:T(8,128)(2,1)} %bitcast.93), calls=%async_computation.6 | async-start | bytes 2621440 | tf_op jit(solution)/shard_map/all_to_all | solution.py:94
  289.4 256.3 %all-reduce.5.cloned.1.call-start = ((), (), s32[]{:S(2)}) async-start(), calls=%async_computation.7 | async-start | bytes 10485760 | tf_op jit(solution)/shard_map/psum | solution.py:107
  291.6 11.0 %copy-start.8 = (bf16[64,5120]{1,0:T(8,128)(2,1)S(1)}, bf16[64,5120]{1,0:T(8,128)(2,1)}, u32[]{:S(2)}) copy-start(bf16[64,5120]{1,0:T(8,128)(2,1)} %param.19) | copy-start | bytes 1966084
  306.6 16.8 %all-to-all-start.4 = ((bf16[8,128,640]{2,1,0:T(8,128)(2,1)}), bf16[8,128,640]{2,1,0:T(8,128)(2,1)S(1)}, u32[]{:S(2)}, u32[]{:S(2)}) async-start(bf16[8,128,640]{2,1,0:T(8,128)(2,1)} %bitcast.87), calls=%async_computation.4 | async-start | bytes 2621440 | tf_op jit(solution)/shard_map/all_to_all | solution.py:92
Sparse Core Ops, SparseCore 0:
  306.7 239.0 all-reduce.4
